TPU v7x, 32 devices: a whole 2x2x4 slice. The times are simulated.
32 devices in a mesh: hst: 4 (over x, core), dev: 8 (over z, y).
Axes of the slice: x: 2, y: 2, z: 4, core: 2. Of those that a mesh axis runs over, the one named last changes fastest.
Arguments:
- features: float32 [524288, 128], P(('hst', 'dev')), may hold values from -6 to 6
- requests: int32 [1024, 256], P(('hst', 'dev')), may hold values from 0 to 16383
- adjacent_one: int32 [135168, 15], P(('hst', 'dev')), may hold values from 0 to 8191, as said below
- adjacent_two: int32 [12288, 10], P(('hst', 'dev')), may hold values from 0 to 4223
- adjacent_three: int32 [2048, 5], P(('hst', 'dev')), may hold values from 0 to 383
- valid_one: int32 [135168, 15], P(('hst', 'dev')), may hold values from 0 to 1, as said below
- valid_two: int32 [12288, 10], P(('hst', 'dev')), may hold values from 0 to 1
- valid_three: int32 [2048, 5], P(('hst', 'dev')), may hold values from 0 to 1
- labels: int32 [2048], P(('hst', 'dev')), may hold values from 0 to 171
- labelled: int32 [2048], P(('hst', 'dev')), may hold values from 0 to 1, as said below
- weights_in: float32 [2, 128, 256], replicated, may hold values from -0.5 to 0.5
- weights_mid: float32 [2, 256, 256], replicated, may hold values from -0.375 to 0.375
- weights_out: float32 [2, 256, 172], replicated, may hold values from -0.375 to 0.375
- biases: float32 [684], replicated, may hold values from -0.6 to 0.6
- moment_one: float32 [684], replicated, may hold values from -0.0007954951 to 0.0007954951
- moment_two: float32 [684], replicated, may hold values from 6.1035155e-07 to 2.4414062e-06
- step_count: int32 [], replicated, may hold values from 2 to 20
- left_in: float32 [2, 128, 128], replicated, as said below
- left_mid: float32 [2, 256, 256], replicated, as said below
- left_out: float32 [2, 256, 256], replicated, as said below
- right_in: float32 [2, 256, 256], replicated, as said below
- right_mid: float32 [2, 256, 256], replicated, as said below
- right_out: float32 [2, 172, 172], replicated, as said below
- invleft_in: float32 [2, 128, 128], replicated, as said below
- invleft_mid: float32 [2, 256, 256], replicated, as said below
- invleft_out: float32 [2, 256, 256], replicated, as said below
- invright_in: float32 [2, 256, 256], replicated, as said below
- invright_mid: float32 [2, 256, 256], replicated, as said below
- invright_out: float32 [2, 172, 172], replicated, as said below
Outputs:
- loss: float32 [], replicated
- new_weights_in: float32 [2, 128, 256], replicated
- new_weights_mid: float32 [2, 256, 256], replicated
- new_weights_out: float32 [2, 256, 172], replicated
- copy_in: bfloat16 [2, 128, 256], replicated
- copy_mid: bfloat16 [2, 256, 256], replicated
- copy_out: bfloat16 [2, 256, 172], replicated
- new_left_in: float32 [2, 128, 128], replicated
- new_left_mid: float32 [2, 256, 256], replicated
- new_left_out: float32 [2, 256, 256], replicated
- new_right_in: float32 [2, 256, 256], replicated
- new_right_mid: float32 [2, 256, 256], replicated
- new_right_out: float32 [2, 172, 172], replicated
- new_biases: float32 [684], replicated
- new_moment_one: float32 [684], replicated
- new_moment_two: float32 [684], replicated
Inputs may be any that keep to these rules, and one draw needn't show every extreme that they name: `adjacent_one`: every one of a device's 8192 pulled slots is named by some entry of its rows. `valid_one`: valid shares differ from device to device. The first seed of every device is labelled. `left_in`: a positive multiple of the identity in each of the two matrices. `left_mid`: a positive multiple of the identity in each of the two matrices. `left_out`: a positive multiple of the identity in each of the two matrices. `right_in`: a positive multiple of the identity in each of the two matrices. `right_mid`: a positive multiple of the identity in each of the two matrices. `right_out`: a positive multiple of the identity in each of the two matrices. `invleft_in`: symmetric. `invleft_mid`: symmetric. `invleft_out`: symmetric. `invright_in`: symmetric. `invright_mid`: symmetric. `invright_out`: symmetric.
All inputs are finite; a program needn't handle non-finite values.
Results may differ from a plain program's by a relative error of at most 0.0094.
Values may be sent and summed in bfloat16 or wider, within the bound.
No kernel may reach another device: no remote copies, remote signals or barrier semaphores. Data moves between devices by JAX's collectives and lax.ppermute only.
A program may use at most 128 MiB of HBM per device.

v0:
```python
import jax
import jax.numpy as jnp
from jax import lax
from jax.sharding import PartitionSpec as P

highest = lax.Precision.HIGHEST


def pull_features(features, requests):
    width = features.shape[1]
    found = features[
        lax.all_to_all(requests, ("hst", "dev"), split_axis=0, concat_axis=0, tiled=True)
    ].astype(jnp.bfloat16)
    arrived = lax.all_to_all(found, ("hst", "dev"), split_axis=0, concat_axis=0, tiled=True)
    return arrived.reshape(-1, width)


def mask_counts(valid_mask):
    weights = valid_mask.astype(jnp.float32)
    return (weights, jnp.maximum(jnp.sum(weights, axis=1), 1.0))


def forward_layer(source, adjacent, valid_mask, weight, bias_row):
    weights, counts = mask_counts(valid_mask)
    summed = jnp.zeros((adjacent.shape[0], source.shape[1]), jnp.float32)
    for column in range(adjacent.shape[1]):
        summed = (
            summed
            + source[adjacent[:, column]].astype(jnp.float32) * weights[:, column : column + 1]
        )
    mixed = (summed / counts[:, None]).astype(jnp.bfloat16)
    selfrows = source[: adjacent.shape[0]]
    preact = (
        jnp.dot(selfrows, weight[0], preferred_element_type=jnp.float32)
        + jnp.dot(mixed, weight[1], preferred_element_type=jnp.float32)
        + bias_row
    )
    return (preact, mixed)


def silu_slope(preact):
    sigma = jax.nn.sigmoid(preact)
    return sigma * (1.0 + preact * (1.0 - sigma))


def contract_rows(left_side, right_side):
    return lax.dot_general(
        left_side, right_side, (((0,), (0,)), ((), ())), preferred_element_type=jnp.float32
    )


def contract_cols(left_side, right_side):
    return lax.dot_general(
        left_side, right_side, (((1,), (1,)), ((), ())), preferred_element_type=jnp.float32
    )


def backward_layer(grad_pre, source, adjacent, valid_mask, mixed, weight, going_down):
    row_count = adjacent.shape[0]
    selfrows = source[:row_count]
    grad_weight = jnp.stack([contract_rows(selfrows, grad_pre), contract_rows(mixed, grad_pre)])
    grad_bias = jnp.sum(grad_pre.astype(jnp.float32), axis=0)
    if not going_down:
        return (grad_weight, grad_bias, None)
    weights, counts = mask_counts(valid_mask)
    to_self = contract_cols(grad_pre, weight[0])
    to_mixed = contract_cols(grad_pre, weight[1]) / counts[:, None]
    grad_source = jnp.zeros(source.shape, jnp.float32).at[:row_count].add(to_self)
    for column in range(adjacent.shape[1]):
        grad_source = grad_source.at[adjacent[:, column]].add(
            to_mixed * weights[:, column : column + 1]
        )
    return (grad_weight, grad_bias, grad_source)


def shampoo(master, gradient, left_stat, right_stat, left_root, right_root):
    left_new = 0.5 * left_stat + 0.5 * jnp.einsum(
        "kio,kjo->kij", gradient, gradient, precision=highest
    )
    right_new = 0.5 * right_stat + 0.5 * jnp.einsum(
        "kio,kip->kop", gradient, gradient, precision=highest
    )
    direction = jnp.einsum("kij,kjo->kio", left_root, gradient, precision=highest)
    direction = jnp.einsum("kio,kop->kip", direction, right_root, precision=highest)
    updated = master - 1.0 * direction
    return (updated, updated.astype(jnp.bfloat16), left_new, right_new)


def adamw(bias_row, gradient, moment_a, moment_b, step_count):
    first_new = 0.9 * moment_a + 0.1 * gradient
    second_new = 0.95 * moment_b + 0.05 * gradient * gradient
    stepped = step_count.astype(jnp.float32)
    first_hat = first_new / (1.0 - 0.9**stepped)
    second_hat = second_new / (1.0 - 0.95**stepped)
    bias_new = bias_row - 0.1 * (first_hat / (jnp.sqrt(second_hat) + 1e-08) + 0.01 * bias_row)
    return (bias_new, first_new, second_new)


def body(
    features,
    requests,
    adjacent_one,
    adjacent_two,
    adjacent_three,
    valid_one,
    valid_two,
    valid_three,
    labels,
    labelled,
    weights_in,
    weights_mid,
    weights_out,
    biases,
    moment_one,
    moment_two,
    step_count,
    left_in,
    left_mid,
    left_out,
    right_in,
    right_mid,
    right_out,
    invleft_in,
    invleft_mid,
    invleft_out,
    invright_in,
    invright_mid,
    invright_out,
):
    pulled = pull_features(features, requests)
    masters = (weights_in, weights_mid, weights_out)
    lowered = [item.astype(jnp.bfloat16) for item in masters]
    widths = [item.shape[2] for item in masters]
    offsets = [0, widths[0], widths[0] + widths[1]]
    bias_rows = [biases[offsets[which] : offsets[which] + widths[which]] for which in range(3)]
    links = ((adjacent_one, valid_one), (adjacent_two, valid_two), (adjacent_three, valid_three))
    sources = [pulled]
    mixes = []
    preacts = []
    for layer_num in range(3):
        preact, mixed = forward_layer(
            sources[-1],
            links[layer_num][0],
            links[layer_num][1],
            lowered[layer_num],
            bias_rows[layer_num],
        )
        mixes.append(mixed)
        preacts.append(preact)
        if layer_num < 2:
            sources.append(jax.nn.silu(preact).astype(jnp.bfloat16))
    marked = labelled.astype(jnp.float32)
    log_total = jax.nn.logsumexp(preact, axis=1)
    onehot = (labels[:, None] == jnp.arange(preact.shape[1], dtype=jnp.int32)[None, :]).astype(
        jnp.float32
    )
    picked = jnp.sum(preact * onehot, axis=1)
    loss_sum = jnp.sum(marked * (log_total - picked))
    grad_pre = (marked[:, None] * (jnp.exp(preact - log_total[:, None]) - onehot)).astype(
        jnp.bfloat16
    )
    grad_weights = [None, None, None]
    grad_biases = [None, None, None]
    for layer_num in (2, 1, 0):
        grad_weight, grad_bias, grad_source = backward_layer(
            grad_pre,
            sources[layer_num],
            links[layer_num][0],
            links[layer_num][1],
            mixes[layer_num],
            lowered[layer_num],
            layer_num > 0,
        )
        grad_weights[layer_num] = grad_weight
        grad_biases[layer_num] = grad_bias
        if layer_num > 0:
            grad_pre = (grad_source * silu_slope(preacts[layer_num - 1])).astype(jnp.bfloat16)
    local_count = jnp.sum(marked)
    grad_in, grad_mid, grad_out, grad_bias_all, loss_total, counted = lax.psum(
        (
            grad_weights[0],
            grad_weights[1],
            grad_weights[2],
            jnp.concatenate(grad_biases),
            loss_sum,
            local_count,
        ),
        ("hst", "dev"),
    )
    loss = loss_total / counted
    out_in = shampoo(weights_in, grad_in / counted, left_in, right_in, invleft_in, invright_in)
    out_mid = shampoo(
        weights_mid, grad_mid / counted, left_mid, right_mid, invleft_mid, invright_mid
    )
    out_out = shampoo(
        weights_out, grad_out / counted, left_out, right_out, invleft_out, invright_out
    )
    bias_new, first_new, second_new = adamw(
        biases, grad_bias_all / counted, moment_one, moment_two, step_count
    )
    return (
        loss,
        out_in[0],
        out_mid[0],
        out_out[0],
        out_in[1],
        out_mid[1],
        out_out[1],
        out_in[2],
        out_mid[2],
        out_out[2],
        out_in[3],
        out_mid[3],
        out_out[3],
        bias_new,
        first_new,
        second_new,
    )


def solution(mesh):
    placed = (
        P(("hst", "dev"), None),
        P(("hst", "dev"), None),
        P(("hst", "dev"), None),
        P(("hst", "dev"), None),
        P(("hst", "dev"), None),
        P(("hst", "dev"), None),
        P(("hst", "dev"), None),
        P(("hst", "dev"), None),
        P(("hst", "dev")),
        P(("hst", "dev")),
        P(),
        P(),
        P(),
        P(),
        P(),
        P(),
        P(),
        P(),
        P(),
        P(),
        P(),
        P(),
        P(),
        P(),
        P(),
        P(),
        P(),
        P(),
        P(),
    )
    return jax.shard_map(
        body,
        mesh=mesh,
        in_specs=placed,
        out_specs=(P(), P(), P(), P(), P(), P(), P(), P(), P(), P(), P(), P(), P(), P(), P(), P()),
        check_vma=False,
    )
```

profile of v0, /device:TPU:0, one launch (start us, length us, event | category | flops | bytes accessed | tf_op | source)
XLA Modules:
  0.0 596.0 jit_solution(15780768578314852755)
XLA Ops:
  8.6 7.3 %all-to-all-start = ((s32[32,1,256]{2,1,0:T(1,128)}), s32[32,1,256]{2,1,0:T(1,128)S(1)}, u32[]{:S(2)}, u32[]{:S(2)}) async-start(s32[32,1,256]{2,1,0:T(1,128)} %all_to_all.11), calls=%async_computation | async-start | bytes 65536 | tf_op jit(solution)/shard_map/all_to_all | solution.py:12
  25.8 31.4 %gather_fusion = bf16[8192,128]{1,0:T(8,128)(2,1)} fusion(f32[16384,128]{1,0:T(8,128)} %param.33, s32[8192]{0:T(1024)S(1)} %broadcast_clamp_fusion), kind=kCustom, calls=%fused_computation | custom fusion | bytes 4227072 | tf_op jit(solution)/shard_map/gather | solution.py:11
  83.9 29.2 %all-to-all-done.1 = bf16[32,256,128]{2,1,0:T(8,128)(2,1)S(1)} async-done(((bf16[32,256,128]{2,1,0:T(8,128)(2,1)}), bf16[32,256,128]{2,1,0:T(8,128)(2,1)S(1)}, u32[]{:S(2)}, u32[]{:S(2)}) %all-to-all-start.1) | async-done | bytes 2097184 | tf_op jit(solution)/shard_map/all_to_all | solution.py:14
  113.1 10.5 %gather_fusion.15 = bf16[4224,128]{1,0:T(8,128)(2,1)} fusion(bf16[8192,128]{1,0:T(8,128)(2,1)S(1)} %bitcast.89, s32[5120]{0:T(1024)} %get-tuple-element.182), kind=kCustom, calls=%fused_computation.15 | custom fusion | bytes 2179584 | tf_op jit(solution)/shard_map/gather | solution.py:29
  123.7 10.5 %gather_fusion.14 = bf16[4224,128]{1,0:T(8,128)(2,1)} fusion(bf16[8192,128]{1,0:T(8,128)(2,1)S(1)} %bitcast.90, s32[5120]{0:T(1024)} %get-tuple-element.183), kind=kCustom, calls=%fused_computation.14 | custom fusion | bytes 2179584 | tf_op jit(solution)/shard_map/gather | solution.py:29
  134.2 9.6 %gather_fusion.13 = bf16[4224,128]{1,0:T(8,128)(2,1)} fusion(bf16[8192,128]{1,0:T(8,128)(2,1)S(1)} %bitcast.91, s32[5120]{0:T(1024)S(1)} %copy-done.25), kind=kCustom, calls=%fused_computation.13 | custom fusion | bytes 2179584 | tf_op jit(solution)/shard_map/gather | solution.py:29
  143.8 9.6 %gather_fusion.12 = bf16[4224,128]{1,0:T(8,128)(2,1)} fusion(bf16[8192,128]{1,0:T(8,128)(2,1)S(1)} %bitcast.92, s32[5120]{0:T(1024)S(1)} %get-tuple-element.185), kind=kCustom, calls=%fused_computation.12 | custom fusion | bytes 2179584 | tf_op jit(solution)/shard_map/gather | solution.py:29
  153.4 10.5 %gather_fusion.11 = bf16[4224,128]{1,0:T(8,128)(2,1)} fusion(bf16[8192,128]{1,0:T(8,128)(2,1)S(1)} %bitcast.93, s32[5120]{0:T(1024)} %get-tuple-element.186), kind=kCustom, calls=%fused_computation.11 | custom fusion | bytes 2179584 | tf_op jit(solution)/shard_map/gather | solution.py:29
  163.9 9.6 %gather_fusion.10 = bf16[4224,128]{1,0:T(8,128)(2,1)} fusion(bf16[8192,128]{1,0:T(8,128)(2,1)S(1)} %bitcast.94, s32[5120]{0:T(1024)S(1)} %copy-done.20), kind=kCustom, calls=%fused_computation.10 | custom fusion | bytes 2179584 | tf_op jit(solution)/shard_map/gather | solution.py:29
  173.5 9.6 %gather_fusion.9 = bf16[4224,128]{1,0:T(8,128)(2,1)} fusion(bf16[8192,128]{1,0:T(8,128)(2,1)S(1)} %bitcast.95, s32[5120]{0:T(1024)S(1)} %copy-done.26), kind=kCustom, calls=%fused_computation.9 | custom fusion | bytes 2179584 | tf_op jit(solution)/shard_map/gather | solution.py:29
  183.0 9.6 %gather_fusion.8 = bf16[4224,128]{1,0:T(8,128)(2,1)} fusion(bf16[8192,128]{1,0:T(8,128)(2,1)S(1)} %bitcast.96, s32[5120]{0:T(1024)S(1)} %copy-done.21), kind=kCustom, calls=%fused_computation.8 | custom fusion | bytes 2179584 | tf_op jit(solution)/shard_map/gather | solution.py:29
  192.6 9.5 %gather_fusion.7 = bf16[4224,128]{1,0:T(8,128)(2,1)} fusion(bf16[8192,128]{1,0:T(8,128)(2,1)S(1)} %bitcast.97, s32[5120]{0:T(1024)S(1)} %copy-done.27), kind=kCustom, calls=%fused_computation.7 | custom fusion | bytes 2179584 | tf_op jit(solution)/shard_map/gather | solution.py:29
  202.2 9.6 %gather_fusion.6 = bf16[4224,128]{1,0:T(8,128)(2,1)} fusion(bf16[8192,128]{1,0:T(8,128)(2,1)S(1)} %bitcast.98, s32[5120]{0:T(1024)S(1)} %copy-done.22), kind=kCustom, calls=%fused_computation.6 | custom fusion | bytes 2179584 | tf_op jit(solution)/shard_map/gather | solution.py:29
  211.8 9.6 %gather_fusion.5 = bf16[4224,128]{1,0:T(8,128)(2,1)} fusion(bf16[8192,128]{1,0:T(8,128)(2,1)S(1)} %bitcast.99, s32[5120]{0:T(1024)S(1)} %copy-done.28), kind=kCustom, calls=%fused_computation.5 | custom fusion | bytes 2179584 | tf_op jit(solution)/shard_map/gather | solution.py:29
  221.4 9.6 %gather_fusion.4 = bf16[4224,128]{1,0:T(8,128)(2,1)} fusion(bf16[8192,128]{1,0:T(8,128)(2,1)S(1)} %bitcast.100, s32[5120]{0:T(1024)S(1)} %copy-done.23), kind=kCustom, calls=%fused_computation.4 | custom fusion | bytes 2179584 | tf_op jit(solution)/shard_map/gather | solution.py:29
  231.0 9.6 %gather_fusion.3 = bf16[4224,128]{1,0:T(8,128)(2,1)} fusion(bf16[8192,128]{1,0:T(8,128)(2,1)S(1)} %bitcast.101, s32[5120]{0:T(1024)S(1)} %copy-done.29), kind=kCustom, calls=%fused_computation.3 | custom fusion | bytes 2179584 | tf_op jit(solution)/shard_map/gather | solution.py:29
  240.5 9.6 %gather_fusion.2 = bf16[4224,128]{1,0:T(8,128)(2,1)} fusion(bf16[8192,128]{1,0:T(8,128)(2,1)S(1)} %bitcast.102, s32[5120]{0:T(1024)S(1)} %copy-done.24), kind=kCustom, calls=%fused_computation.2 | custom fusion | bytes 2179584 | tf_op jit(solution)/shard_map/gather | solution.py:29
  250.1 9.6 %gather_fusion.1 = bf16[4224,128]{1,0:T(8,128)(2,1)} fusion(bf16[8192,128]{1,0:T(8,128)(2,1)S(1)} %bitcast.103, s32[5120]{0:T(1024)S(1)} %copy-done.30), kind=kCustom, calls=%fused_computation.1 | custom fusion | bytes 2179584 | tf_op jit(solution)/shard_map/gather | solution.py:29
  262.2 13.4 %divide_convert_fusion = bf16[4224,128]{1,0:T(8,128)(2,1)S(1)} fusion(bf16[4224,128]{1,0:T(8,128)(2,1)S(1)} %copy-done.1, bf16[4224,128]{1,0:T(8,128)(2,1)S(1)} %copy-done.2, bf16[4224,128]{1,0:T(8,128)(2,1)S(1)} %copy-done.3, bf16[4224,128]{1,0:T(8,128)(2,1)S(1)} %copy-done.4, bf16[4224,128]{1,0:T(8,128)(2,1)S(1)} %copy-done.5, ...), kind=kLoop, calls=%fused_computation.52 | loop fusion | flops 24870912 | bytes 17571840 | tf_op jit(solution)/shard_map/convert_element_type | solution.py:31
  353.6 7.3 %scatter_custom_fusion.5 = f32[4224,256]{1,0:T(8,128)} fusion(f32[4224,256]{1,0:T(8,128)} %scatter-add.121, s32[384]{0:T(512)} %copy-done.68, f32[384,256]{1,0:T(8,128)S(1)} %convolution_divide_fusion, f32[384]{0:T(512)S(1)} %copy-done.42), kind=kCustom, calls=%fused_computation.103 | custom fusion | flops 196608 | bytes 4720128 | tf_op jit(solution)/shard_map/scatter-add | solution.py:70
  360.9 6.9 %scatter_custom_fusion.6 = f32[4224,256]{1,0:T(8,128)} fusion(f32[4224,256]{1,0:T(8,128)} %scatter_custom_fusion.5, s32[384]{0:T(512)} %copy-done.67, f32[384,256]{1,0:T(8,128)S(1)} %convolution_divide_fusion, f32[384]{0:T(512)S(1)} %copy-done.40), kind=kCustom, calls=%fused_computation.101 | custom fusion | flops 196608 | bytes 4720128 | tf_op jit(solution)/shard_map/scatter-add | solution.py:70
  395.2 7.0 %scatter_custom_fusion.11 = f32[4224,256]{1,0:T(8,128)} fusion(f32[4224,256]{1,0:T(8,128)} %scatter_custom_fusion.10, s32[384]{0:T(512)} %copy-done.62, f32[384,256]{1,0:T(8,128)S(1)} %convolution_divide_fusion, f32[384]{0:T(512)S(1)} %copy-done.34), kind=kCustom, calls=%fused_computation.91 | custom fusion | flops 196608 | bytes 4720128 | tf_op jit(solution)/shard_map/scatter-add | solution.py:70
  432.5 37.9 %all-reduce.2 = (f32[]{:T(128)}, f32[]{:T(128)}, f32[684]{0:T(1024)S(1)}) all-reduce(f32[]{:T(128)} %get-tuple-element.141, f32[]{:T(128)} %get-tuple-element.140, f32[684]{0:T(1024)S(1)} %pad_maximum_fusion.3), channel_id=1, replica_groups=mesh['hst'=4,'dev'=8] {'hst','dev'}, use_global_device_ids=true, to_apply=%region_7.8 | all-reduce | flops 686 | bytes 5488 | tf_op jit(solution)/shard_map/psum | solution.py:179
  473.0 88.9 %all-reduce.6.cloned.1.call-done = (f32[2,128,256]{2,1,0:T(8,128)}, f32[2,256,256]{2,1,0:T(8,128)}, f32[2,256,172]{1,2,0:T(8,128)}) async-done(((f32[2,128,256]{2,1,0:T(8,128)}, f32[2,256,256]{2,1,0:T(8,128)}, f32[2,256,172]{1,2,0:T(8,128)}), (f32[2,128,256]{2,1,0:T(8,128)}, f32[2,256,256]{2,1,0:T(8,128)}, f32[2,256,172]{1,2,0:T(8,128)})) %all-reduce.6.cloned.1.call-update) | async-done | bytes 1138704 | tf_op jit(solution)/shard_map/psum | solution.py:179
  (297 shorter events, 201.9 us)
Async XLA Ops:
  7.2 579.1 %copy-start = (f32[2,256,256]{2,1,0:T(8,128)S(1)}, f32[2,256,256]{2,1,0:T(8,128)}, u32[]{:S(2)}) copy-start(f32[2,256,256]{2,1,0:T(8,128)} %param.60) | copy-start | bytes 1572868
  8.6 17.1 %all-to-all-start = ((s32[32,1,256]{2,1,0:T(1,128)}), s32[32,1,256]{2,1,0:T(1,128)S(1)}, u32[]{:S(2)}, u32[]{:S(2)}) async-start(s32[32,1,256]{2,1,0:T(1,128)} %all_to_all.11), calls=%async_computation | async-start | bytes 65536 | tf_op jit(solution)/shard_map/all_to_all | solution.py:12
  57.2 15.0 %copy-start.19 = (s32[384,10]{0,1:T(8,128)S(1)}, s32[384,10]{0,1:T(8,128)}, u32[]{:S(2)}) copy-start(s32[384,10]{0,1:T(8,128)} %param.39) | copy-start | bytes 46084
  57.2 21.0 %copy-start.10 = (s32[4224,15]{0,1:T(8,128)S(1)}, s32[4224,15]{0,1:T(8,128)}, u32[]{:S(2)}) copy-start(s32[4224,15]{0,1:T(8,128)} %param.38) | copy-start | bytes 760324
  57.2 55.9 %all-to-all-start.1 = ((bf16[32,256,128]{2,1,0:T(8,128)(2,1)}), bf16[32,256,128]{2,1,0:T(8,128)(2,1)S(1)}, u32[]{:S(2)}, u32[]{:S(2)}) async-start(bf16[32,256,128]{2,1,0:T(8,128)(2,1)} %bitcast.106), calls=%async_computation.1 | async-start | bytes 4194304 | tf_op jit(solution)/shard_map/all_to_all | solution.py:14
  63.1 498.9 %all-reduce.6.cloned.1.call-start = ((), (), s32[]{:S(2)}) async-start(), calls=%async_computation.2 | async-start | bytes 2293760 | tf_op jit(solution)/shard_map/psum | solution.py:179
  63.1 19.0 %copy-start.44 = (f32[684]{0:T(1024)S(1)}, f32[684]{0:T(1024)}, u32[]{:S(2)}) copy-start(f32[684]{0:T(1024)} %param.46) | copy-start | bytes 8212
  63.1 19.6 %copy-start.46 = (f32[64,5]{0,1:T(8,128)S(1)}, f32[64,5]{0,1:T(8,128)}, u32[]{:S(2)}) copy-start(f32[64,5]{0,1:T(8,128)} %convert_element_type.201) | copy-start | bytes 3844
  123.7 10.5 %copy-start.25 = (s32[5120]{0:T(1024)S(1)}, s32[5120]{0:T(1024)}, u32[]{:S(2)}) copy-start(s32[5120]{0:T(1024)} %get-tuple-element.184) | copy-start | bytes 61444
  153.4 10.5 %copy-start.20 = (s32[5120]{0:T(1024)S(1)}, s32[5120]{0:T(1024)}, u32[]{:S(2)}) copy-start(s32[5120]{0:T(1024)} %get-tuple-element.187) | copy-start | bytes 61444
  163.9 9.6 %copy-start.26 = (s32[5120]{0:T(1024)S(1)}, s32[5120]{0:T(1024)}, u32[]{:S(2)}) copy-start(s32[5120]{0:T(1024)} %get-tuple-element.188) | copy-start | bytes 61444
  173.5 9.6 %copy-start.21 = (s32[5120]{0:T(1024)S(1)}, s32[5120]{0:T(1024)}, u32[]{:S(2)}) copy-start(s32[5120]{0:T(1024)} %get-tuple-element.189) | copy-start | bytes 61444
  183.0 9.6 %copy-start.27 = (s32[5120]{0:T(1024)S(1)}, s32[5120]{0:T(1024)}, u32[]{:S(2)}) copy-start(s32[5120]{0:T(1024)} %get-tuple-element.190) | copy-start | bytes 61444
  202.2 9.6 %copy-start.28 = (s32[5120]{0:T(1024)S(1)}, s32[5120]{0:T(1024)}, u32[]{:S(2)}) copy-start(s32[5120]{0:T(1024)} %get-tuple-element.192) | copy-start | bytes 61444
  221.4 9.6 %copy-start.29 = (s32[5120]{0:T(1024)S(1)}, s32[5120]{0:T(1024)}, u32[]{:S(2)}) copy-start(s32[5120]{0:T(1024)} %get-tuple-element.194) | copy-start | bytes 61444
  231.0 9.6 %copy-start.24 = (s32[5120]{0:T(1024)S(1)}, s32[5120]{0:T(1024)}, u32[]{:S(2)}) copy-start(s32[5120]{0:T(1024)} %get-tuple-element.195) | copy-start | bytes 61444
  240.5 9.6 %copy-start.30 = (s32[5120]{0:T(1024)S(1)}, s32[5120]{0:T(1024)}, u32[]{:S(2)}) copy-start(s32[5120]{0:T(1024)} %pad_clamp_fusion.14) | copy-start | bytes 61444
  429.3 42.4 %copy-start.45 = (f32[684]{0:T(1024)S(1)}, f32[684]{0:T(1024)}, u32[]{:S(2)}) copy-start(f32[684]{0:T(1024)} %param.46) | copy-start | bytes 8212
  429.3 42.4 %copy-start.71 = (f32[684]{0:T(1024)S(1)}, f32[684]{0:T(1024)}, u32[]{:S(2)}) copy-start(f32[684]{0:T(1024)} %param.48) | copy-start | bytes 8212
  429.3 42.4 %copy-start.72 = (f32[684]{0:T(1024)S(1)}, f32[684]{0:T(1024)}, u32[]{:S(2)}) copy-start(f32[684]{0:T(1024)} %param.47) | copy-start | bytes 8212
  429.4 132.6 %copy-start.88 = (f32[2,128,128]{2,1,0:T(8,128)S(1)}, f32[2,128,128]{2,1,0:T(8,128)}, u32[]{:S(2)}) copy-start(f32[2,128,128]{2,1,0:T(8,128)} %param.50) | copy-start | bytes 393220
  429.4 135.4 %copy-start.89 = (f32[2,128,128]{2,1,0:T(8,128)S(1)}, f32[2,128,128]{2,1,0:T(8,128)}, u32[]{:S(2)}) copy-start(f32[2,128,128]{2,1,0:T(8,128)} %param.56) | copy-start | bytes 393220
  430.1 136.6 %copy-start.16 = (f32[2,256,256]{2,1,0:T(8,128)S(1)}, f32[2,256,256]{2,1,0:T(8,128)}, u32[]{:S(2)}) copy-start(f32[2,256,256]{2,1,0:T(8,128)} %param.53) | copy-start | bytes 1572868
  431.7 138.3 %copy-start.87 = (f32[2,172,172]{2,0,1:T(2,128)S(1)}, f32[2,172,172]{2,0,1:T(2,128)}, u32[]{:S(2)}) copy-start(f32[2,172,172]{2,0,1:T(2,128)} %param.55) | copy-start | bytes 710020
  (69 other events, 358.1 us)
Sparse Core Ops, SparseCore 0:
  431.8 130.0 all-reduce.5
where the time goes:
time: 602 us; the launch traced here: 596 us
  local copies, waits for them, and re-layouts  242 us (40%)
  other arithmetic  128 us (21%)
  waiting for transfers between devices  118 us (20%)
  matrix products  38.9 us (6%)
  blocking collectives  37.9 us (6%)
  between operations  18.5 us (3%)
  starting transfers between devices  13.2 us (2%)
    gather x30, local copies, waits for them, and re-layouts, forward_layer(): source[adjacent[:, column]].astype(jnp.float32)  193 us
    psum x1, waiting for transfers between devices, body(): lax.psum((grad_weights[0], grad_weights[1], grad_weights[2], jnp.concaten...  88.9 us
    scatter-add x15, other arithmetic, backward_layer(): grad_source.at[adjacent[:, column]]  75.7 us
    psum x1, blocking collectives, body(): lax.psum((grad_weights[0], grad_weights[1], grad_weights[2], jnp.concaten...  37.9 us
    gather x1, local copies, waits for them, and re-layouts, pull_features(): features[lax.all_to_all(requests, ('hst', 'dev'), split_axis=0, concat_ax...  31.4 us
    all_to_all x1, waiting for transfers between devices, pull_features(): lax.all_to_all(found, ('hst', 'dev'), split_axis=0, concat_axis=0, tiled=...  29.2 us
    convert_element_type x3, other arithmetic, forward_layer(): mixed = (summed / counts[:, None]).astype(jnp.bfloat16)  16.5 us
  transfers between devices with their start and end apart: 3, of which 2 were waited for; matrix products, arithmetic and copies ran while one was open for 5% of the time, Pallas kernels for 0%

commit v1 on v0

--- a/solution.py
+++ b/solution.py
@@ -176,7 +176,12 @@
         if layer_num > 0:
             grad_pre = (grad_source * silu_slope(preacts[layer_num - 1])).astype(jnp.bfloat16)
     local_count = jnp.sum(marked)
-    grad_in, grad_mid, grad_out, grad_bias_all, loss_total, counted = lax.psum(
+
+    def manage_the_spans(u):
+        a_next = lax.psum(lax.psum(u, "hst"), "dev")
+        return a_next
+
+    grad_in, grad_mid, grad_out, grad_bias_all, loss_total, counted = manage_the_spans(
         (
             grad_weights[0],
             grad_weights[1],
@@ -184,8 +189,7 @@
             jnp.concatenate(grad_biases),
             loss_sum,
             local_count,
-        ),
-        ("hst", "dev"),
+        )
     )
     loss = loss_total / counted
     out_in = shampoo(weights_in, grad_in / counted, left_in, right_in, invleft_in, invright_in)

time: 602 us -> 593 us (0.985)
  blocking collectives: 37.9 us -> 29.4 us
    psum x1 -> x2, blocking collectives: 37.9 us -> 29.4 us  [manage_the_spans(): a_next = lax.psum(lax.psum(u, 'hst'), 'dev')]
    psum x1 -> x2, waiting for transfers between devices: 88.9 us -> 87.4 us  [manage_the_spans(): a_next = lax.psum(lax.psum(u, 'hst'), 'dev')]
  transfers between devices with their start and end apart: 3 -> 4, of which waited for: 2 -> 3; matrix products, arithmetic and copies ran while one was open for 5% -> 5% of each run, Pallas kernels for 0% -> 0%
where the time goes in v1:
time: 593 us; the launch traced here: 586 us
  local copies, waits for them, and re-layouts  242 us (41%)
  other arithmetic  128 us (22%)
  waiting for transfers between devices  117 us (20%)
  matrix products  38.9 us (7%)
  blocking collectives  29.4 us (5%)
  between operations  18.5 us (3%)
  starting transfers between devices  13.2 us (2%)
    gather x30, local copies, waits for them, and re-layouts, forward_layer(): source[adjacent[:, column]].astype(jnp.float32)  193 us
    psum x2, waiting for transfers between devices, manage_the_spans(): a_next = lax.psum(lax.psum(u, 'hst'), 'dev')  87.4 us
    scatter-add x15, other arithmetic, backward_layer(): grad_source.at[adjacent[:, column]]  75.7 us
    gather x1, local copies, waits for them, and re-layouts, pull_features(): features[lax.all_to_all(requests, ('hst', 'dev'), split_axis=0, concat_ax...  31.4 us
    psum x2, blocking collectives, manage_the_spans(): a_next = lax.psum(lax.psum(u, 'hst'), 'dev')  29.4 us
    all_to_all x1, waiting for transfers between devices, pull_features(): lax.all_to_all(found, ('hst', 'dev'), split_axis=0, concat_axis=0, tiled=...  29.2 us
    convert_element_type x3, other arithmetic, forward_layer(): mixed = (summed / counts[:, None]).astype(jnp.bfloat16)  16.5 us
  transfers between devices with their start and end apart: 4, of which 3 were waited for; matrix products, arithmetic and copies ran while one was open for 5% of the time, Pallas kernels for 0%

profile of v1, /device:TPU:0, one launch (start us, length us, event | category | flops | bytes accessed | tf_op | source)
XLA Modules:
  0.0 586.2 jit_solution(13890578351511449130)
XLA Ops:
  8.6 7.3 %all-to-all-start = ((s32[32,1,256]{2,1,0:T(1,128)}), s32[32,1,256]{2,1,0:T(1,128)S(1)}, u32[]{:S(2)}, u32[]{:S(2)}) async-start(s32[32,1,256]{2,1,0:T(1,128)} %all_to_all.11), calls=%async_computation | async-start | bytes 65536 | tf_op jit(solution)/shard_map/all_to_all | solution.py:12
  25.8 31.4 %gather_fusion = bf16[8192,128]{1,0:T(8,128)(2,1)} fusion(f32[16384,128]{1,0:T(8,128)} %param.33, s32[8192]{0:T(1024)S(1)} %broadcast_clamp_fusion), kind=kCustom, calls=%fused_computation | custom fusion | bytes 4227072 | tf_op jit(solution)/shard_map/gather | solution.py:11
  83.9 29.2 %all-to-all-done.1 = bf16[32,256,128]{2,1,0:T(8,128)(2,1)S(1)} async-done(((bf16[32,256,128]{2,1,0:T(8,128)(2,1)}), bf16[32,256,128]{2,1,0:T(8,128)(2,1)S(1)}, u32[]{:S(2)}, u32[]{:S(2)}) %all-to-all-start.1) | async-done | bytes 2097184 | tf_op jit(solution)/shard_map/all_to_all | solution.py:14
  113.1 10.5 %gather_fusion.15 = bf16[4224,128]{1,0:T(8,128)(2,1)} fusion(bf16[8192,128]{1,0:T(8,128)(2,1)S(1)} %bitcast.89, s32[5120]{0:T(1024)} %get-tuple-element.188), kind=kCustom, calls=%fused_computation.15 | custom fusion | bytes 2179584 | tf_op jit(solution)/shard_map/gather | solution.py:29
  123.7 10.5 %gather_fusion.14 = bf16[4224,128]{1,0:T(8,128)(2,1)} fusion(bf16[8192,128]{1,0:T(8,128)(2,1)S(1)} %bitcast.90, s32[5120]{0:T(1024)} %get-tuple-element.189), kind=kCustom, calls=%fused_computation.14 | custom fusion | bytes 2179584 | tf_op jit(solution)/shard_map/gather | solution.py:29
  134.2 9.6 %gather_fusion.13 = bf16[4224,128]{1,0:T(8,128)(2,1)} fusion(bf16[8192,128]{1,0:T(8,128)(2,1)S(1)} %bitcast.91, s32[5120]{0:T(1024)S(1)} %copy-done.25), kind=kCustom, calls=%fused_computation.13 | custom fusion | bytes 2179584 | tf_op jit(solution)/shard_map/gather | solution.py:29
  143.8 9.6 %gather_fusion.12 = bf16[4224,128]{1,0:T(8,128)(2,1)} fusion(bf16[8192,128]{1,0:T(8,128)(2,1)S(1)} %bitcast.92, s32[5120]{0:T(1024)S(1)} %get-tuple-element.191), kind=kCustom, calls=%fused_computation.12 | custom fusion | bytes 2179584 | tf_op jit(solution)/shard_map/gather | solution.py:29
  153.4 10.5 %gather_fusion.11 = bf16[4224,128]{1,0:T(8,128)(2,1)} fusion(bf16[8192,128]{1,0:T(8,128)(2,1)S(1)} %bitcast.93, s32[5120]{0:T(1024)} %get-tuple-element.192), kind=kCustom, calls=%fused_computation.11 | custom fusion | bytes 2179584 | tf_op jit(solution)/shard_map/gather | solution.py:29
  163.9 9.6 %gather_fusion.10 = bf16[4224,128]{1,0:T(8,128)(2,1)} fusion(bf16[8192,128]{1,0:T(8,128)(2,1)S(1)} %bitcast.94, s32[5120]{0:T(1024)S(1)} %copy-done.20), kind=kCustom, calls=%fused_computation.10 | custom fusion | bytes 2179584 | tf_op jit(solution)/shard_map/gather | solution.py:29
  173.5 9.6 %gather_fusion.9 = bf16[4224,128]{1,0:T(8,128)(2,1)} fusion(bf16[8192,128]{1,0:T(8,128)(2,1)S(1)} %bitcast.95, s32[5120]{0:T(1024)S(1)} %copy-done.26), kind=kCustom, calls=%fused_computation.9 | custom fusion | bytes 2179584 | tf_op jit(solution)/shard_map/gather | solution.py:29
  183.0 9.6 %gather_fusion.8 = bf16[4224,128]{1,0:T(8,128)(2,1)} fusion(bf16[8192,128]{1,0:T(8,128)(2,1)S(1)} %bitcast.96, s32[5120]{0:T(1024)S(1)} %copy-done.21), kind=kCustom, calls=%fused_computation.8 | custom fusion | bytes 2179584 | tf_op jit(solution)/shard_map/gather | solution.py:29
  192.6 9.5 %gather_fusion.7 = bf16[4224,128]{1,0:T(8,128)(2,1)} fusion(bf16[8192,128]{1,0:T(8,128)(2,1)S(1)} %bitcast.97, s32[5120]{0:T(1024)S(1)} %copy-done.27), kind=kCustom, calls=%fused_computation.7 | custom fusion | bytes 2179584 | tf_op jit(solution)/shard_map/gather | solution.py:29
  202.2 9.6 %gather_fusion.6 = bf16[4224,128]{1,0:T(8,128)(2,1)} fusion(bf16[8192,128]{1,0:T(8,128)(2,1)S(1)} %bitcast.98, s32[5120]{0:T(1024)S(1)} %copy-done.22), kind=kCustom, calls=%fused_computation.6 | custom fusion | bytes 2179584 | tf_op jit(solution)/shard_map/gather | solution.py:29
  211.8 9.6 %gather_fusion.5 = bf16[4224,128]{1,0:T(8,128)(2,1)} fusion(bf16[8192,128]{1,0:T(8,128)(2,1)S(1)} %bitcast.99, s32[5120]{0:T(1024)S(1)} %copy-done.28), kind=kCustom, calls=%fused_computation.5 | custom fusion | bytes 2179584 | tf_op jit(solution)/shard_map/gather | solution.py:29
  221.4 9.6 %gather_fusion.4 = bf16[4224,128]{1,0:T(8,128)(2,1)} fusion(bf16[8192,128]{1,0:T(8,128)(2,1)S(1)} %bitcast.100, s32[5120]{0:T(1024)S(1)} %copy-done.23), kind=kCustom, calls=%fused_computation.4 | custom fusion | bytes 2179584 | tf_op jit(solution)/shard_map/gather | solution.py:29
  231.0 9.6 %gather_fusion.3 = bf16[4224,128]{1,0:T(8,128)(2,1)} fusion(bf16[8192,128]{1,0:T(8,128)(2,1)S(1)} %bitcast.101, s32[5120]{0:T(1024)S(1)} %copy-done.29), kind=kCustom, calls=%fused_computation.3 | custom fusion | bytes 2179584 | tf_op jit(solution)/shard_map/gather | solution.py:29
  240.5 9.6 %gather_fusion.2 = bf16[4224,128]{1,0:T(8,128)(2,1)} fusion(bf16[8192,128]{1,0:T(8,128)(2,1)S(1)} %bitcast.102, s32[5120]{0:T(1024)S(1)} %copy-done.24), kind=kCustom, calls=%fused_computation.2 | custom fusion | bytes 2179584 | tf_op jit(solution)/shard_map/gather | solution.py:29
  250.1 9.6 %gather_fusion.1 = bf16[4224,128]{1,0:T(8,128)(2,1)} fusion(bf16[8192,128]{1,0:T(8,128)(2,1)S(1)} %bitcast.103, s32[5120]{0:T(1024)S(1)} %copy-done.30), kind=kCustom, calls=%fused_computation.1 | custom fusion | bytes 2179584 | tf_op jit(solution)/shard_map/gather | solution.py:29
  262.2 13.4 %divide_convert_fusion = bf16[4224,128]{1,0:T(8,128)(2,1)S(1)} fusion(bf16[4224,128]{1,0:T(8,128)(2,1)S(1)} %copy-done.1, bf16[4224,128]{1,0:T(8,128)(2,1)S(1)} %copy-done.2, bf16[4224,128]{1,0:T(8,128)(2,1)S(1)} %copy-done.3, bf16[4224,128]{1,0:T(8,128)(2,1)S(1)} %copy-done.4, bf16[4224,128]{1,0:T(8,128)(2,1)S(1)} %copy-done.5, ...), kind=kLoop, calls=%fused_computation.52 | loop fusion | flops 24870912 | bytes 17571840 | tf_op jit(solution)/shard_map/convert_element_type | solution.py:31
  353.6 7.3 %scatter_custom_fusion.5 = f32[4224,256]{1,0:T(8,128)} fusion(f32[4224,256]{1,0:T(8,128)} %scatter-add.121, s32[384]{0:T(512)} %copy-done.68, f32[384,256]{1,0:T(8,128)S(1)} %convolution_divide_fusion, f32[384]{0:T(512)S(1)} %copy-done.42), kind=kCustom, calls=%fused_computation.103 | custom fusion | flops 196608 | bytes 4720128 | tf_op jit(solution)/shard_map/scatter-add | solution.py:70
  395.2 7.0 %scatter_custom_fusion.11 = f32[4224,256]{1,0:T(8,128)} fusion(f32[4224,256]{1,0:T(8,128)} %scatter_custom_fusion.10, s32[384]{0:T(512)} %copy-done.62, f32[384,256]{1,0:T(8,128)S(1)} %convolution_divide_fusion, f32[384]{0:T(512)S(1)} %copy-done.34), kind=kCustom, calls=%fused_computation.91 | custom fusion | flops 196608 | bytes 4720128 | tf_op jit(solution)/shard_map/scatter-add | solution.py:70
  431.8 35.3 %all-reduce.11.cloned.1.call-done = (f32[2,128,256]{2,1,0:T(8,128)}, f32[2,256,256]{2,1,0:T(8,128)}, f32[2,256,172]{1,2,0:T(8,128)}) async-done(((f32[2,128,256]{2,1,0:T(8,128)}, f32[2,256,256]{2,1,0:T(8,128)}, f32[2,256,172]{1,2,0:T(8,128)}), (f32[2,128,256]{2,1,0:T(8,128)}, f32[2,256,256]{2,1,0:T(8,128)}, f32[2,256,172]{1,2,0:T(8,128)})) %all-reduce.11.cloned.1.call-update) | async-done | bytes 1138704 | tf_op jit(solution)/shard_map/psum | solution.py:181
  474.7 22.6 %all-reduce.2 = (f32[]{:T(128)}, f32[]{:T(128)}, f32[684]{0:T(1024)S(1)}) all-reduce(f32[]{:T(128)} %get-tuple-element.148, f32[]{:T(128)} %get-tuple-element.149, f32[684]{0:T(1024)S(1)} %get-tuple-element.150), channel_id=1, replica_groups=mesh['hst'=4,'dev'=8] {'dev'}, use_global_device_ids=true, to_apply=%region_8.9 | all-reduce | flops 686 | bytes 5488 | tf_op jit(solution)/shard_map/psum | solution.py:181
  500.0 52.1 %all-reduce.9.cloned.1.call-done = (f32[2,128,256]{2,1,0:T(8,128)}, f32[2,256,256]{2,1,0:T(8,128)}, f32[2,256,172]{1,2,0:T(8,128)}) async-done(((f32[2,128,256]{2,1,0:T(8,128)}, f32[2,256,256]{2,1,0:T(8,128)}, f32[2,256,172]{1,2,0:T(8,128)}), (f32[2,128,256]{2,1,0:T(8,128)}, f32[2,256,256]{2,1,0:T(8,128)}, f32[2,256,172]{1,2,0:T(8,128)})) %all-reduce.9.cloned.1.call-update) | async-done | bytes 1138704 | tf_op jit(solution)/shard_map/psum | solution.py:181
  (301 shorter events, 215.6 us)
Async XLA Ops:
  7.2 569.3 %copy-start = (f32[2,256,256]{2,1,0:T(8,128)S(1)}, f32[2,256,256]{2,1,0:T(8,128)}, u32[]{:S(2)}) copy-start(f32[2,256,256]{2,1,0:T(8,128)} %param.60) | copy-start | bytes 1572868
  8.6 17.1 %all-to-all-start = ((s32[32,1,256]{2,1,0:T(1,128)}), s32[32,1,256]{2,1,0:T(1,128)S(1)}, u32[]{:S(2)}, u32[]{:S(2)}) async-start(s32[32,1,256]{2,1,0:T(1,128)} %all_to_all.11), calls=%async_computation | async-start | bytes 65536 | tf_op jit(solution)/shard_map/all_to_all | solution.py:12
  57.2 15.0 %copy-start.19 = (s32[384,10]{0,1:T(8,128)S(1)}, s32[384,10]{0,1:T(8,128)}, u32[]{:S(2)}) copy-start(s32[384,10]{0,1:T(8,128)} %param.39) | copy-start | bytes 46084
  57.2 21.0 %copy-start.10 = (s32[4224,15]{0,1:T(8,128)S(1)}, s32[4224,15]{0,1:T(8,128)}, u32[]{:S(2)}) copy-start(s32[4224,15]{0,1:T(8,128)} %param.38) | copy-start | bytes 760324
  57.2 55.9 %all-to-all-start.1 = ((bf16[32,256,128]{2,1,0:T(8,128)(2,1)}), bf16[32,256,128]{2,1,0:T(8,128)(2,1)S(1)}, u32[]{:S(2)}, u32[]{:S(2)}) async-start(bf16[32,256,128]{2,1,0:T(8,128)(2,1)} %bitcast.106), calls=%async_computation.1 | async-start | bytes 4194304 | tf_op jit(solution)/shard_map/all_to_all | solution.py:14
  63.1 404.0 %all-reduce.11.cloned.1.call-start = ((), (), s32[]{:S(2)}) async-start(), calls=%async_computation.3 | async-start | bytes 2293760 | tf_op jit(solution)/shard_map/psum | solution.py:181
  63.1 19.0 %copy-start.44 = (f32[684]{0:T(1024)S(1)}, f32[684]{0:T(1024)}, u32[]{:S(2)}) copy-start(f32[684]{0:T(1024)} %param.46) | copy-start | bytes 8212
  63.1 19.6 %copy-start.46 = (f32[64,5]{0,1:T(8,128)S(1)}, f32[64,5]{0,1:T(8,128)}, u32[]{:S(2)}) copy-start(f32[64,5]{0,1:T(8,128)} %convert_element_type.201) | copy-start | bytes 3844
  123.7 10.5 %copy-start.25 = (s32[5120]{0:T(1024)S(1)}, s32[5120]{0:T(1024)}, u32[]{:S(2)}) copy-start(s32[5120]{0:T(1024)} %get-tuple-element.190) | copy-start | bytes 61444
  153.4 10.5 %copy-start.20 = (s32[5120]{0:T(1024)S(1)}, s32[5120]{0:T(1024)}, u32[]{:S(2)}) copy-start(s32[5120]{0:T(1024)} %get-tuple-element.193) | copy-start | bytes 61444
  163.9 9.6 %copy-start.26 = (s32[5120]{0:T(1024)S(1)}, s32[5120]{0:T(1024)}, u32[]{:S(2)}) copy-start(s32[5120]{0:T(1024)} %get-tuple-element.194) | copy-start | bytes 61444
  183.0 9.6 %copy-start.27 = (s32[5120]{0:T(1024)S(1)}, s32[5120]{0:T(1024)}, u32[]{:S(2)}) copy-start(s32[5120]{0:T(1024)} %get-tuple-element.196) | copy-start | bytes 61444
  202.2 9.6 %copy-start.28 = (s32[5120]{0:T(1024)S(1)}, s32[5120]{0:T(1024)}, u32[]{:S(2)}) copy-start(s32[5120]{0:T(1024)} %get-tuple-element.198) | copy-start | bytes 61444
  221.4 9.6 %copy-start.29 = (s32[5120]{0:T(1024)S(1)}, s32[5120]{0:T(1024)}, u32[]{:S(2)}) copy-start(s32[5120]{0:T(1024)} %get-tuple-element.200) | copy-start | bytes 61444
  429.3 38.6 %copy-start.69 = (f32[172]{0:T(256)S(1)}, f32[172]{0:T(256)}, u32[]{:S(2)}) copy-start(f32[172]{0:T(256)} %get-tuple-element.161) | copy-start | bytes 2068
  429.3 38.6 %copy-start.70 = (f32[256]{0:T(256)S(1)}, f32[256]{0:T(256)}, u32[]{:S(2)}) copy-start(f32[256]{0:T(256)} %get-tuple-element.159) | copy-start | bytes 3076
  429.3 69.4 %copy-start.45 = (f32[684]{0:T(1024)S(1)}, f32[684]{0:T(1024)}, u32[]{:S(2)}) copy-start(f32[684]{0:T(1024)} %param.46) | copy-start | bytes 8212
  429.3 69.4 %copy-start.71 = (f32[684]{0:T(1024)S(1)}, f32[684]{0:T(1024)}, u32[]{:S(2)}) copy-start(f32[684]{0:T(1024)} %param.48) | copy-start | bytes 8212
  429.3 69.4 %copy-start.72 = (f32[684]{0:T(1024)S(1)}, f32[684]{0:T(1024)}, u32[]{:S(2)}) copy-start(f32[684]{0:T(1024)} %param.47) | copy-start | bytes 8212
  430.1 122.0 %copy-start.88 = (f32[2,128,128]{2,1,0:T(8,128)S(1)}, f32[2,128,128]{2,1,0:T(8,128)}, u32[]{:S(2)}) copy-start(f32[2,128,128]{2,1,0:T(8,128)} %param.50) | copy-start | bytes 393220
  431.0 124.0 %copy-start.89 = (f32[2,128,128]{2,1,0:T(8,128)S(1)}, f32[2,128,128]{2,1,0:T(8,128)}, u32[]{:S(2)}) copy-start(f32[2,128,128]{2,1,0:T(8,128)} %param.56) | copy-start | bytes 393220
  431.7 125.3 %copy-start.16 = (f32[2,256,256]{2,1,0:T(8,128)S(1)}, f32[2,256,256]{2,1,0:T(8,128)}, u32[]{:S(2)}) copy-start(f32[2,256,256]{2,1,0:T(8,128)} %param.53) | copy-start | bytes 1572868
  431.7 120.4 %all-reduce.9.cloned.1.call-start = ((), (), s32[]{:S(2)}) async-start(), calls=%async_computation.2 | async-start | bytes 2293760 | tf_op jit(solution)/shard_map/psum | solution.py:181
  467.1 93.1 %copy-start.87 = (f32[2,172,172]{2,0,1:T(2,128)S(1)}, f32[2,172,172]{2,0,1:T(2,128)}, u32[]{:S(2)}) copy-start(f32[2,172,172]{2,0,1:T(2,128)} %param.55) | copy-start | bytes 710020
  (70 other events, 380.5 us)
Sparse Core Ops, SparseCore 0:
  431.8 35.2 all-reduce.10
  470.9 81.1 all-reduce.8
